TPU v7x, 512 devices: a whole 4x4x16 slice. The times are simulated.
512 devices in a mesh: len: 128 (over y, z, core), pipe: 4 (over x).
Axes of the slice: x: 4, y: 4, z: 16, core: 2. Of those that a mesh axis runs over, the one named last changes fastest.
Arguments:
- inputs: bfloat16 [512, 2048, 256], P(('len', 'pipe')), may hold values from -6 to 6
- cotangent: bfloat16 [512, 2048, 256], P(('len', 'pipe')), may hold values from -6 to 6
- point_weight: bfloat16 [256, 256], replicated, may hold values from -0.375 to 0.375
- point_bias: float32 [256], replicated, may hold values from -3 to 3
- spec_real: bfloat16 [128, 256, 256], P('len'), may hold values from -0.25 to 0.25
- spec_imag: bfloat16 [128, 256, 256], P('len'), may hold values from -0.25 to 0.25
- junc_weight: bfloat16 [256, 256], replicated, may hold values from -0.375 to 0.375
- junc_bias: float32 [256], replicated, may hold values from -3 to 3
- inlet_ids: int32 [512], replicated, may hold values from 0 to 511
- outlet_ids: int32 [512], replicated, may hold values from 0 to 511
Outputs:
- outputs: bfloat16 [512, 2048, 256], P(('len', 'pipe'))
- grad_inputs: bfloat16 [512, 2048, 256], P(('len', 'pipe'))
- grad_real: float32 [128, 256, 256], P('len')
- grad_imag: float32 [128, 256, 256], P('len')
All inputs are finite; a program needn't handle non-finite values.
Results may differ from a plain program's by a relative error of at most 0.015.
Values may be sent and summed in bfloat16 or wider, within the bound.
A program may use at most 64 MiB of HBM per device.

v0:
```python
import math
import jax
import jax.numpy as jnp
from jax import lax
from jax.sharding import PartitionSpec as P

COUPLING = 0.125


def tables(cell_count, mode_count):
    position = lax.broadcasted_iota(jnp.int32, (mode_count, cell_count), 1)
    frequency = lax.broadcasted_iota(jnp.int32, (mode_count, cell_count), 0)
    product_index = frequency * position % cell_count
    angles = product_index.astype(jnp.float32) * (2.0 * math.pi / cell_count)
    norm_scale = 1.0 / math.sqrt(cell_count)
    cosine = jnp.cos(angles) * norm_scale
    sine_table = jnp.sin(angles) * norm_scale
    doubled = jnp.where(frequency == 0, 1.0, 2.0)
    forward = (
        jnp.stack([cosine, -sine_table], axis=1)
        .reshape(2 * mode_count, cell_count)
        .astype(jnp.bfloat16)
    )
    inverse = jnp.transpose(
        jnp.stack([doubled * cosine, -doubled * sine_table], axis=1).reshape(
            2 * mode_count, cell_count
        )
    ).astype(jnp.bfloat16)
    return (forward, inverse)


def spectral_blocks(spec_real, spec_imag):
    upper = jnp.concatenate([spec_real, spec_imag], axis=2)
    lower = jnp.concatenate([-spec_imag, spec_real], axis=2)
    return jnp.concatenate([upper, lower], axis=1)


def activate(values):
    return jax.nn.gelu(values, approximate=True)


def silu_slope(values):
    sigmoid_part = jax.nn.sigmoid(values)
    return sigmoid_part * (1.0 + values * (1.0 - sigmoid_part))


def to_modes(field):
    return lax.all_to_all(field, "len", split_axis=1, concat_axis=0, tiled=True)


def from_modes(field):
    return lax.all_to_all(field, "len", split_axis=0, concat_axis=1, tiled=True)


def body(
    inputs,
    cotangent,
    point_weight,
    point_bias,
    spec_real,
    spec_imag,
    junc_weight,
    junc_bias,
    inlet_ids,
    outlet_ids,
):
    per_dev, cell_count, channels = inputs.shape
    len_count = lax.axis_size("len")
    mode_count = spec_real.shape[0] * len_count
    junc_count = inlet_ids.shape[0]
    forward, inverse = tables(cell_count, mode_count)
    blocks = spectral_blocks(spec_real, spec_imag)
    start = (lax.axis_index("len") * lax.axis_size("pipe") + lax.axis_index("pipe")) * per_dev
    my_inlets = lax.dynamic_slice_in_dim(inlet_ids, start, per_dev)
    my_outlets = lax.dynamic_slice_in_dim(outlet_ids, start, per_dev)
    mine = jnp.concatenate([my_inlets, my_outlets])[:, None]
    in_match = mine == inlet_ids[None, :]
    out_match = mine == outlet_ids[None, :]
    end_rows = lax.all_gather(
        jnp.stack([inputs[:, 0, :], inputs[:, -1, :]]), ("len", "pipe"), axis=1, tiled=True
    )
    spectra = jnp.einsum("kl,plc->pkc", forward, inputs, preferred_element_type=jnp.float32).astype(
        jnp.bfloat16
    )
    mode_rows = to_modes(spectra.reshape(per_dev, mode_count, 2, channels))
    mode_rows = mode_rows.reshape(mode_rows.shape[0], -1, 2 * channels)
    mixed = jnp.einsum(
        "pmk,mkn->pmn", mode_rows, blocks, preferred_element_type=jnp.float32
    ).astype(jnp.bfloat16)
    returned_modes = from_modes(mixed.reshape(mixed.shape[0], -1, 2, channels)).reshape(
        per_dev, 2 * mode_count, channels
    )
    junc_sums = jnp.dot(
        in_match.astype(jnp.bfloat16), end_rows[0], preferred_element_type=jnp.float32
    ) + jnp.dot(out_match.astype(jnp.bfloat16), end_rows[1], preferred_element_type=jnp.float32)
    junc_act = (
        jnp.dot(junc_sums.astype(jnp.bfloat16), junc_weight, preferred_element_type=jnp.float32)
        + junc_bias
    )
    junc_rows = jax.nn.silu(junc_act).astype(jnp.bfloat16).astype(jnp.float32)
    cond = COUPLING * (junc_rows[:per_dev] + junc_rows[per_dev:])
    spectral = jnp.einsum(
        "lk,pkc->plc", inverse, returned_modes, preferred_element_type=jnp.float32
    )
    pre = (spectral + cond[:, None, :]).astype(jnp.bfloat16)
    pointwise = jnp.dot(
        inputs.reshape(-1, channels), point_weight, preferred_element_type=jnp.float32
    ).reshape(inputs.shape)
    summed = pointwise + point_bias + pre.astype(jnp.float32)
    result, pullback = jax.vjp(activate, summed)
    outputs = result.astype(jnp.bfloat16)
    grad_total = pullback(cotangent.astype(jnp.float32))[0].astype(jnp.bfloat16)
    grad_spec = jnp.einsum(
        "lk,plc->pkc", inverse, grad_total, preferred_element_type=jnp.float32
    ).astype(jnp.bfloat16)
    grad_modes = to_modes(grad_spec.reshape(per_dev, mode_count, 2, channels))
    grad_modes = grad_modes.reshape(grad_modes.shape[0], -1, 2 * channels)
    grad_mixed = jnp.einsum(
        "pmn,mkn->pmk", grad_modes, blocks, preferred_element_type=jnp.float32
    ).astype(jnp.bfloat16)
    weight_terms = jnp.einsum(
        "pmk,pmn->mkn", mode_rows, grad_modes, preferred_element_type=jnp.float32
    )
    real_terms = weight_terms[:, :channels, :channels] + weight_terms[:, channels:, channels:]
    imag_terms = weight_terms[:, :channels, channels:] - weight_terms[:, channels:, :channels]
    grad_real, grad_imag = (
        jnp.sum(
            lax.all_gather(real_terms.astype(jnp.bfloat16), "pipe").astype(jnp.float32), axis=0
        ),
        jnp.sum(
            lax.all_gather(imag_terms.astype(jnp.bfloat16), "pipe").astype(jnp.float32), axis=0
        ),
    )
    grad_back = from_modes(grad_mixed.reshape(grad_mixed.shape[0], -1, 2, channels)).reshape(
        per_dev, 2 * mode_count, channels
    )
    grad_cells = jnp.einsum("kl,pkc->plc", forward, grad_back, preferred_element_type=jnp.float32)
    grad_cond = jnp.sum(grad_total, axis=1, dtype=jnp.float32)
    all_cond = lax.all_gather(grad_cond, ("len", "pipe"), axis=0, tiled=True)
    junc_grad = COUPLING * jnp.dot(
        in_match.astype(jnp.float32) + out_match.astype(jnp.float32),
        all_cond,
        precision=lax.Precision.HIGHEST,
    )
    act_grad = (junc_grad * silu_slope(junc_act)).astype(jnp.bfloat16)
    sums_grad = jnp.dot(act_grad, junc_weight.T, preferred_element_type=jnp.float32).astype(
        jnp.bfloat16
    )
    end_first = sums_grad[:per_dev].astype(jnp.float32)
    end_last = sums_grad[per_dev:].astype(jnp.float32)
    grad_cells = grad_cells.at[:, 0, :].add(end_first).at[:, -1, :].add(end_last)
    spread = grad_cells.astype(jnp.bfloat16)
    grad_local = jnp.dot(
        grad_total.reshape(-1, channels), point_weight.T, preferred_element_type=jnp.float32
    ).reshape(inputs.shape)
    grad_inputs = (grad_local + spread.astype(jnp.float32)).astype(jnp.bfloat16)
    return (outputs, grad_inputs, grad_real, grad_imag)


def solution(mesh):
    placed = (
        P(("len", "pipe"), None, None),
        P(("len", "pipe"), None, None),
        P(),
        P(),
        P("len", None, None),
        P("len", None, None),
        P(),
        P(),
        P(),
        P(),
    )
    return jax.shard_map(
        body,
        mesh=mesh,
        in_specs=placed,
        out_specs=(
            P(("len", "pipe"), None, None),
            P(("len", "pipe"), None, None),
            P("len", None, None),
            P("len", None, None),
        ),
        check_vma=False,
    )
```

profile of v0, /device:TPU:16, one launch (start us, length us, event | category | flops | bytes accessed | tf_op | source)
XLA Modules:
  0.0 529.5 jit_solution(12464476966603268177)
XLA Ops:
  0.6 0.0 copy-start
  0.6 4.3 negate_convert_fusion
  5.0 0.1 pad_maximum_fusion
  5.1 0.0 copy-start.3
  5.1 1.1 copy.48
  6.2 0.0 copy-start.10
  6.2 0.0 copy-start.11
  6.2 0.4 convert_element_type.155
  6.7 0.0 copy-start.6
  6.7 0.4 fusion.18
  7.1 0.7 reshape.318
  7.8 19.7 %all-to-all-start = ((bf16[1,128,2,256]{3,2,0,1:T(2,128)(2,1)}), bf16[1,128,2,256]{3,2,0,1:T(2,128)(2,1)S(1)}, u32[]{:S(2)}, u32[]{:S(2)}) async-start(bf16[1,128,2,256]{3,2,0,1:T(2,128)(2,1)} %bitcast.6), calls=%async_computation | async-start | bytes 262144 | tf_op jit(solution)/shard_map/all_to_all | solution.py:48
  27.6 0.6 dynamic_slice.6
  28.2 0.6 dynamic_slice.7
  28.8 0.0 copy-start.8
  28.8 1.4 pad_add_fusion
  30.2 4.4 multiply_convert_fusion.1
  34.6 0.0 copy-start.15
  34.6 0.1 pad_maximum_fusion.1
  34.7 195.5 %all_gather.18 = bf16[2,512,256]{2,0,1:T(2,128)(2,1)S(1)} all-gather(bf16[2,1,256]{2,0,1:T(2,128)(2,1)S(1)} %pad_maximum_fusion.2), channel_id=1, replica_groups=mesh['len'=128,'pipe'=4] {'len','pipe'}, dimensions={1}, use_global_device_ids=true | all-gather | bytes 525312 | tf_op jit(solution)/shard_map/all_gather | solution.py:79
  230.3 1.5 fusion.64
  231.8 0.0 all-to-all-done
  231.8 0.3 convolution_convert_fusion.1
  232.2 0.8 copy.50
  233.0 16.1 %all-to-all-start.1 = ((bf16[128,1,2,256]{3,2,1,0:T(2,128)(2,1)}), bf16[128,1,2,256]{3,2,1,0:T(2,128)(2,1)}, u32[]{:S(2)}, u32[]{:S(2)}) async-start(bf16[128,1,2,256]{3,2,1,0:T(2,128)(2,1)} %copy.50), calls=%async_computation.1 | async-start | bytes 262144 | tf_op jit(solution)/shard_map/all_to_all | solution.py:52
  249.1 0.8 fusion.39
  249.8 1.1 copy.51
  250.9 0.4 convert_element_type.163
  251.4 0.0 copy-start.4
  251.4 1.5 fusion.54
  252.9 12.6 %all-to-all-done.1 = bf16[128,1,2,256]{3,2,1,0:T(2,128)(2,1)} async-done(((bf16[128,1,2,256]{3,2,1,0:T(2,128)(2,1)}), bf16[128,1,2,256]{3,2,1,0:T(2,128)(2,1)}, u32[]{:S(2)}, u32[]{:S(2)}) %all-to-all-start.1) | async-done | bytes 131104 | tf_op jit(solution)/shard_map/all_to_all | solution.py:52
  265.5 1.0 reshape.321
  266.4 0.0 copy-start.14
  266.5 0.6 fusion.7
  267.0 0.6 copy-done.14
  267.7 3.7 convert_reduce_fusion
  271.4 1.0 copy-done.1
  272.3 0.4 fusion.19
  272.8 0.7 reshape.324
  273.5 7.5 %all-to-all-start.2 = ((bf16[1,128,2,256]{3,2,0,1:T(2,128)(2,1)}), bf16[1,128,2,256]{3,2,0,1:T(2,128)(2,1)S(1)}, u32[]{:S(2)}, u32[]{:S(2)}) async-start(bf16[1,128,2,256]{3,2,0,1:T(2,128)(2,1)} %bitcast.19), calls=%async_computation.2 | async-start | bytes 262144 | tf_op jit(solution)/shard_map/all_to_all | solution.py:48
  281.0 194.3 %all-gather.3 = f32[512,1,256]{2,1,0:T(1,128)S(1)} all-gather(f32[1,1,256]{2,1,0:T(1,128)S(1)} %bitcast.136), channel_id=2, replica_groups=mesh['len'=128,'pipe'=4] {'len','pipe'}, dimensions={0}, use_global_device_ids=true | all-gather | bytes 525312 | tf_op jit(solution)/shard_map/all_gather | solution.py:139
  475.3 0.3 fusion.22
  475.6 0.0 copy-done.5
  475.7 0.1 convolution_convert_fusion.4
  475.8 0.0 all-to-all-done.2
  475.9 0.3 convolution_convert_fusion
  476.2 0.3 convolution_bitcast_fusion.2
  476.5 0.8 copy.58
  477.3 15.6 %all-to-all-start.3 = ((bf16[128,1,2,256]{3,2,1,0:T(2,128)(2,1)}), bf16[128,1,2,256]{3,2,1,0:T(2,128)(2,1)S(1)}, u32[]{:S(2)}, u32[]{:S(2)}) async-start(bf16[128,1,2,256]{3,2,1,0:T(2,128)(2,1)} %copy.58), calls=%async_computation.3 | async-start | bytes 262144 | tf_op jit(solution)/shard_map/all_to_all | solution.py:52
  492.9 0.1 fusion.37
  493.0 12.8 %all-gather.1 = bf16[4,256,256]{2,1,0:T(8,128)(2,1)S(1)} all-gather(bf16[1,256,256]{2,1,0:T(8,128)(2,1)S(1)} %get-tuple-element.32), channel_id=3, replica_groups=mesh['len'=128,'pipe'=4] {'pipe'}, dimensions={0}, use_global_device_ids=true | all-gather | bytes 655360 | tf_op jit(solution)/shard_map/all_gather | solution.py:128
  505.8 0.8 convert_reduce_fusion.2
  506.5 13.4 %all-gather.2 = bf16[4,256,256]{2,1,0:T(8,128)(2,1)S(1)} all-gather(bf16[1,256,256]{2,1,0:T(8,128)(2,1)S(1)} %get-tuple-element.31), channel_id=4, replica_groups=mesh['len'=128,'pipe'=4] {'pipe'}, dimensions={0}, use_global_device_ids=true | all-gather | bytes 655360 | tf_op jit(solution)/shard_map/all_gather | solution.py:131
  519.9 0.8 convert_reduce_fusion.1
  520.7 0.0 all-to-all-done.3
  520.7 0.1 reshape.327
  520.8 0.5 fusion.67
  521.2 0.1 slice_reduce_fusion
  521.3 0.0 copy-start.2
  521.3 1.8 copy.59
  523.2 1.3 scatter-add.6
  524.5 0.7 fusion.56
  525.2 1.3 scatter-add.9
  526.5 3.0 fusion.4
  (30 shorter events, 0.2 us)
Async XLA Ops:
  0.6 266.4 %copy-start = (bf16[256,256]{1,0:T(8,128)(2,1)S(1)}, bf16[256,256]{1,0:T(8,128)(2,1)}, u32[]{:S(2)}) copy-start(bf16[256,256]{1,0:T(8,128)(2,1)} %param.16) | copy-start | bytes 393220
  5.1 1.6 copy-start.3
  6.2 21.4 %copy-start.10 = (s32[512]{0:T(512)S(1)}, s32[512]{0:T(512)}, u32[]{:S(2)}) copy-start(s32[512]{0:T(512)} %param.22) | copy-start | bytes 6148
  6.2 22.0 %copy-start.11 = (s32[512]{0:T(512)S(1)}, s32[512]{0:T(512)}, u32[]{:S(2)}) copy-start(s32[512]{0:T(512)} %param.23) | copy-start | bytes 6148
  6.7 22.1 %copy-start.6 = (bf16[1,256,256]{2,1,0:T(8,128)(2,1)S(1)}, bf16[1,256,256]{2,1,0:T(8,128)(2,1)}, u32[]{:S(2)}) copy-start(bf16[1,256,256]{2,1,0:T(8,128)(2,1)} %param.19) | copy-start | bytes 393220
  7.8 223.9 %all-to-all-start = ((bf16[1,128,2,256]{3,2,0,1:T(2,128)(2,1)}), bf16[1,128,2,256]{3,2,0,1:T(2,128)(2,1)S(1)}, u32[]{:S(2)}, u32[]{:S(2)}) async-start(bf16[1,128,2,256]{3,2,0,1:T(2,128)(2,1)} %bitcast.6), calls=%async_computation | async-start | bytes 262144 | tf_op jit(solution)/shard_map/all_to_all | solution.py:48
  28.8 203.0 %copy-start.8 = (bf16[1,256,256]{2,1,0:T(8,128)(2,1)}, bf16[1,256,256]{2,1,0:T(8,128)(2,1)S(1)}, u32[]{:S(2)}) copy-start(bf16[1,256,256]{2,1,0:T(8,128)(2,1)S(1)} %neg.22) | copy-start | bytes 393220
  30.2 221.1 %copy-start.12 = (s32[2]{0:T(128)}, s32[2]{0:T(128)S(1)}, u32[]{:S(2)}) copy-start(s32[2]{0:T(128)S(1)} %pad_add_fusion) | copy-start | bytes 28
  34.6 197.2 %copy-start.15 = (bf16[1,256,256]{2,1,0:T(8,128)(2,1)S(1)}, bf16[1,256,256]{2,1,0:T(8,128)(2,1)}, u32[]{:S(2)}) copy-start(bf16[1,256,256]{2,1,0:T(8,128)(2,1)} %param.18) | copy-start | bytes 393220
  233.0 32.5 %all-to-all-start.1 = ((bf16[128,1,2,256]{3,2,1,0:T(2,128)(2,1)}), bf16[128,1,2,256]{3,2,1,0:T(2,128)(2,1)}, u32[]{:S(2)}, u32[]{:S(2)}) async-start(bf16[128,1,2,256]{3,2,1,0:T(2,128)(2,1)} %copy.50), calls=%async_computation.1 | async-start | bytes 262144 | tf_op jit(solution)/shard_map/all_to_all | solution.py:52
  251.4 15.7 %copy-start.4 = (bf16[1,2048,256]{2,1,0:T(8,128)(2,1)S(1)}, bf16[1,2048,256]{2,1,0:T(8,128)(2,1)}, u32[]{:S(2)}) copy-start(bf16[1,2048,256]{2,1,0:T(8,128)(2,1)} %param.14) | copy-start | bytes 3145732
  266.4 1.2 copy-start.14
  271.3 1.0 copy-start.1
  271.3 204.0 %copy-start.13 = (s32[2]{0:T(128)S(1)}, s32[2]{0:T(128)}, u32[]{:S(2)}) copy-start(s32[2]{0:T(128)} %copy-done.12) | copy-start | bytes 28
  271.4 204.3 %copy-start.5 = (bf16[256,256]{1,0:T(8,128)(2,1)S(1)}, bf16[256,256]{1,0:T(8,128)(2,1)}, u32[]{:S(2)}) copy-start(bf16[256,256]{1,0:T(8,128)(2,1)} %param.20) | copy-start | bytes 393220
  272.3 203.6 %copy-start.7 = (bf16[1,256,256]{2,1,0:T(8,128)(2,1)S(1)}, bf16[1,256,256]{2,1,0:T(8,128)(2,1)}, u32[]{:S(2)}) copy-start(bf16[1,256,256]{2,1,0:T(8,128)(2,1)} %param.19) | copy-start | bytes 393220
  272.3 203.6 %copy-start.9 = (bf16[1,256,256]{2,1,0:T(8,128)(2,1)S(1)}, bf16[1,256,256]{2,1,0:T(8,128)(2,1)}, u32[]{:S(2)}) copy-start(bf16[1,256,256]{2,1,0:T(8,128)(2,1)} %copy-done.8) | copy-start | bytes 393220
  272.3 203.6 %copy-start.16 = (bf16[1,256,256]{2,1,0:T(8,128)(2,1)S(1)}, bf16[1,256,256]{2,1,0:T(8,128)(2,1)}, u32[]{:S(2)}) copy-start(bf16[1,256,256]{2,1,0:T(8,128)(2,1)} %param.18) | copy-start | bytes 393220
  273.5 202.3 %all-to-all-start.2 = ((bf16[1,128,2,256]{3,2,0,1:T(2,128)(2,1)}), bf16[1,128,2,256]{3,2,0,1:T(2,128)(2,1)S(1)}, u32[]{:S(2)}, u32[]{:S(2)}) async-start(bf16[1,128,2,256]{3,2,0,1:T(2,128)(2,1)} %bitcast.19), calls=%async_computation.2 | async-start | bytes 262144 | tf_op jit(solution)/shard_map/all_to_all | solution.py:48
  477.3 43.4 %all-to-all-start.3 = ((bf16[128,1,2,256]{3,2,1,0:T(2,128)(2,1)}), bf16[128,1,2,256]{3,2,1,0:T(2,128)(2,1)S(1)}, u32[]{:S(2)}, u32[]{:S(2)}) async-start(bf16[128,1,2,256]{3,2,1,0:T(2,128)(2,1)} %copy.58), calls=%async_computation.3 | async-start | bytes 262144 | tf_op jit(solution)/shard_map/all_to_all | solution.py:52
  521.3 5.2 copy-start.2
where the time goes:
time: 530 us
  blocking collectives  416 us (78%)
  starting transfers between devices  58.9 us (11%)
  local copies, waits for them, and re-layouts  16.1 us (3%)
  other arithmetic  12.6 us (2%)
  waiting for transfers between devices  12.6 us (2%)
  matrix products  12.3 us (2%)
    all_gather x1, blocking collectives, body(): lax.all_gather(jnp.stack([inputs[:, 0, :], inputs[:, -1, :]]), ('len', 'p...  196 us
    all_gather x1, blocking collectives, body(): all_cond = lax.all_gather(grad_cond, ('len', 'pipe'), axis=0, tiled=True)  194 us
    all_to_all x2, starting transfers between devices, from_modes(): return lax.all_to_all(field, 'len', split_axis=0, concat_axis=1, tiled=True)  31.7 us
    all_to_all x2, starting transfers between devices, to_modes(): return lax.all_to_all(field, 'len', split_axis=1, concat_axis=0, tiled=True)  27.2 us
    all_gather x1, blocking collectives, body(): lax.all_gather(imag_terms.astype(jnp.bfloat16), 'pipe').astype(jnp.float32)  13.4 us
    all_gather x1, blocking collectives, body(): lax.all_gather(real_terms.astype(jnp.bfloat16), 'pipe').astype(jnp.float32)  12.8 us
    all_to_all x2, waiting for transfers between devices, from_modes(): return lax.all_to_all(field, 'len', split_axis=0, concat_axis=1, tiled=True)  12.6 us
  transfers between devices with their start and end apart: 4, of which 1 were waited for; matrix products, arithmetic and copies ran while one was open for 3% of the time, Pallas kernels for 0%

commit v1 on v0

--- a/solution.py
+++ b/solution.py
@@ -136,7 +136,12 @@
     )
     grad_cells = jnp.einsum("kl,pkc->plc", forward, grad_back, preferred_element_type=jnp.float32)
     grad_cond = jnp.sum(grad_total, axis=1, dtype=jnp.float32)
-    all_cond = lax.all_gather(grad_cond, ("len", "pipe"), axis=0, tiled=True)
+    all_cond = jnp.concatenate(
+        lax.all_to_all(
+            jnp.stack([grad_cond] * lax.axis_size(("len", "pipe"))), ("len", "pipe"), 0, 0
+        ),
+        axis=0,
+    )
     junc_grad = COUPLING * jnp.dot(
         in_match.astype(jnp.float32) + out_match.astype(jnp.float32),
         all_cond,

time: 530 us -> 379 us (0.72)
  the two profiles are of different devices: /device:TPU:16 before, /device:TPU:1 now
where the time goes in v1:
time: 379 us; the launch traced here: 378 us
  blocking collectives  270 us (71%)
  starting transfers between devices  47.7 us (13%)
  waiting for transfers between devices  18.3 us (5%)
  local copies, waits for them, and re-layouts  15.8 us (4%)
  matrix products  13.3 us (4%)
  other arithmetic  12.6 us (3%)
    all_gather x1, blocking collectives, body(): lax.all_gather(jnp.stack([inputs[:, 0, :], inputs[:, -1, :]]), ('len', 'p...  197 us
    all_to_all x1, blocking collectives, to_modes(): return lax.all_to_all(field, 'len', split_axis=1, concat_axis=0, tiled=True)  23.8 us
    all_to_all x1, blocking collectives, from_modes(): return lax.all_to_all(field, 'len', split_axis=0, concat_axis=1, tiled=True)  23.8 us
    all_to_all x1, starting transfers between devices, to_modes(): return lax.all_to_all(field, 'len', split_axis=1, concat_axis=0, tiled=True)  20.6 us
    all_to_all x1, starting transfers between devices, from_modes(): return lax.all_to_all(field, 'len', split_axis=0, concat_axis=1, tiled=True)  14.4 us
    all_to_all x1, waiting for transfers between devices, from_modes(): return lax.all_to_all(field, 'len', split_axis=0, concat_axis=1, tiled=True)  13.1 us
    all_gather x1, blocking collectives, body(): lax.all_gather(real_terms.astype(jnp.bfloat16), 'pipe').astype(jnp.float32)  13 us
    all_to_all x1, starting transfers between devices, body(): lax.all_to_all(jnp.stack([grad_cond] * lax.axis_size(('len', 'pipe'))), (...  12.7 us
  transfers between devices with their start and end apart: 3, of which 2 were waited for; matrix products, arithmetic and copies ran while one was open for 4% of the time, Pallas kernels for 0%

profile of v1, /device:TPU:1, one launch (start us, length us, event | category | flops | bytes accessed | tf_op | source)
XLA Modules:
  0.0 378.4 jit_solution(18236571204453687937)
XLA Ops:
  0.6 0.0 copy-start
  0.6 4.3 %negate_convert_fusion = (bf16[128,1,2048]{2,0,1:T(8,128)(2,1)S(1)}, bf16[128,1,2048]{2,0,1:T(8,128)(2,1)S(1)}) fusion(), kind=kLoop, calls=%fused_computation.57 | loop fusion | flops 4980736 | bytes 1048576 | tf_op jit(solution)/shard_map/convert.6
  5.0 0.1 pad_maximum_fusion
  5.1 0.0 copy-start.3
  5.1 1.1 copy.48
  6.2 0.0 copy-start.10
  6.2 0.0 copy-start.11
  6.2 0.4 convert_element_type.155
  6.7 0.0 copy-start.5
  6.7 0.4 fusion.18
  7.1 0.7 reshape.324
  7.8 20.6 %all-to-all-start = ((bf16[1,128,2,256]{3,2,0,1:T(2,128)(2,1)}), bf16[1,128,2,256]{3,2,0,1:T(2,128)(2,1)S(1)}, u32[]{:S(2)}, u32[]{:S(2)}) async-start(bf16[1,128,2,256]{3,2,0,1:T(2,128)(2,1)} %bitcast.6), calls=%async_computation | async-start | bytes 262144 | tf_op jit(solution)/shard_map/all_to_all | solution.py:48
  28.5 0.6 dynamic_slice.6
  29.1 0.6 dynamic_slice.7
  29.7 0.0 copy-start.8
  29.7 1.4 pad_add_fusion
  31.1 4.4 %multiply_convert_fusion.1 = (bf16[128,1,2048]{2,0,1:T(8,128)(2,1)S(1)}, bf16[128,1,2048]{2,0,1:T(8,128)(2,1)S(1)}) fusion(f32[128]{0:T(128)S(1)} %negate_multiply_fusion, f32[128]{0:T(128)S(1)} %fusion.60), kind=kLoop, calls=%fused_computation.55 | loop fusion | flops 4718592 | bytes 1049600 | tf_op jit(solution)/shard_map/convert.4
  35.5 0.0 copy-start.15
  35.5 0.1 pad_maximum_fusion.1
  35.6 197.2 %all_gather.15 = bf16[2,512,256]{2,0,1:T(2,128)(2,1)S(1)} all-gather(bf16[2,1,256]{2,0,1:T(2,128)(2,1)S(1)} %pad_maximum_fusion.2), channel_id=1, replica_groups=mesh['len'=128,'pipe'=4] {'len','pipe'}, dimensions={1}, use_global_device_ids=true | all-gather | bytes 525312 | tf_op jit(solution)/shard_map/all_gather | solution.py:79
  232.8 1.5 fusion.64
  234.4 0.3 convolution_convert_fusion.1
  234.7 0.8 copy.50
  235.5 14.4 %all-to-all-start.1 = ((bf16[128,1,2,256]{3,2,1,0:T(2,128)(2,1)}), bf16[128,1,2,256]{3,2,1,0:T(2,128)(2,1)}, u32[]{:S(2)}, u32[]{:S(2)}) async-start(bf16[128,1,2,256]{3,2,1,0:T(2,128)(2,1)} %copy.50), calls=%async_computation.1 | async-start | bytes 262144 | tf_op jit(solution)/shard_map/all_to_all | solution.py:52
  249.9 0.8 fusion.39
  250.7 1.1 copy.51
  251.8 0.4 convert_element_type.163
  252.2 0.0 copy-start.4
  252.2 1.5 fusion.54
  253.8 13.1 %all-to-all-done.1 = bf16[128,1,2,256]{3,2,1,0:T(2,128)(2,1)} async-done(((bf16[128,1,2,256]{3,2,1,0:T(2,128)(2,1)}), bf16[128,1,2,256]{3,2,1,0:T(2,128)(2,1)}, u32[]{:S(2)}, u32[]{:S(2)}) %all-to-all-start.1) | async-done | bytes 131104 | tf_op jit(solution)/shard_map/all_to_all | solution.py:52
  266.8 1.0 reshape.327
  267.8 0.0 copy-start.14
  267.8 0.6 fusion.7
  268.4 0.6 copy-done.14
  269.0 3.7 convert_reduce_fusion
  272.7 1.0 copy-done.1
  273.7 0.4 fusion.19
  274.1 0.1 reshape.330
  274.2 23.8 %all_to_all.20 = bf16[1,128,2,256]{3,2,0,1:T(2,128)(2,1)S(1)} all-to-all(bf16[1,128,2,256]{3,2,0,1:T(2,128)(2,1)S(1)} %bitcast.128), channel_id=1, replica_groups=mesh['len'=128,'pipe'=4] {'len'}, dimensions={1} | all-to-all | bytes 262144 | tf_op jit(solution)/shard_map/all_to_all | solution.py:48
  298.1 0.3 convolution_convert_fusion
  298.4 0.1 copy.58
  298.5 23.8 %all_to_all.42 = bf16[128,1,2,256]{3,2,1,0:T(2,128)(2,1)S(1)} all-to-all(bf16[128,1,2,256]{3,2,1,0:T(2,128)(2,1)S(1)} %copy.58), channel_id=1, replica_groups=mesh['len'=128,'pipe'=4] {'len'}, dimensions={0} | all-to-all | bytes 262144 | tf_op jit(solution)/shard_map/all_to_all | solution.py:52
  322.3 1.1 stack.13
  323.4 12.7 %all-to-all-start.4 = ((f32[512,1,256]{2,1,0:T(1,128)}), f32[512,1,256]{2,1,0:T(1,128)}, u32[]{:S(2)}, u32[]{:S(2)}) async-start(f32[512,1,256]{2,1,0:T(1,128)} %stack.13), calls=%async_computation.4 | async-start | bytes 1048576 | tf_op jit(solution)/shard_map/all_to_all | solution.py:140
  336.1 0.3 convolution_bitcast_fusion.2
  336.4 0.1 fusion.37
  336.5 13.0 %all-gather = bf16[4,256,256]{2,1,0:T(8,128)(2,1)S(1)} all-gather(bf16[1,256,256]{2,1,0:T(8,128)(2,1)S(1)} %get-tuple-element.32), channel_id=2, replica_groups=mesh['len'=128,'pipe'=4] {'pipe'}, dimensions={0}, use_global_device_ids=true | all-gather | bytes 655360 | tf_op jit(solution)/shard_map/all_gather | solution.py:128
  349.5 0.8 convert_reduce_fusion.2
  350.3 11.6 %all-gather.1 = bf16[4,256,256]{2,1,0:T(8,128)(2,1)S(1)} all-gather(bf16[1,256,256]{2,1,0:T(8,128)(2,1)S(1)} %get-tuple-element.31), channel_id=3, replica_groups=mesh['len'=128,'pipe'=4] {'pipe'}, dimensions={0}, use_global_device_ids=true | all-gather | bytes 655360 | tf_op jit(solution)/shard_map/all_gather | solution.py:131
  361.9 0.8 convert_reduce_fusion.1
  362.7 0.1 reshape.333
  362.8 0.5 fusion.67
  363.2 0.0 copy-start.7
  363.2 0.0 copy-start.2
  363.2 1.8 copy.59
  365.1 0.1 slice_reduce_fusion
  365.2 5.2 %all-to-all-done.4 = f32[512,1,256]{2,1,0:T(1,128)} async-done(((f32[512,1,256]{2,1,0:T(1,128)}), f32[512,1,256]{2,1,0:T(1,128)}, u32[]{:S(2)}, u32[]{:S(2)}) %all-to-all-start.4) | async-done | bytes 524320 | tf_op jit(solution)/shard_map/all_to_all | solution.py:140
  370.4 1.4 fusion.22
  371.8 0.0 copy-done.7
  371.8 0.1 convolution_convert_fusion.4
  372.0 1.3 scatter-add.6
  373.3 0.7 fusion.56
  374.0 1.3 scatter-add.9
  375.3 3.0 fusion.4
  (30 shorter events, 0.1 us)
Async XLA Ops:
  0.6 267.8 %copy-start = (bf16[256,256]{1,0:T(8,128)(2,1)S(1)}, bf16[256,256]{1,0:T(8,128)(2,1)}, u32[]{:S(2)}) copy-start(bf16[256,256]{1,0:T(8,128)(2,1)} %param.16) | copy-start | bytes 393220
  5.1 1.6 copy-start.3
  6.2 22.3 %copy-start.10 = (s32[512]{0:T(512)S(1)}, s32[512]{0:T(512)}, u32[]{:S(2)}) copy-start(s32[512]{0:T(512)} %param.22) | copy-start | bytes 6148
  6.2 22.9 %copy-start.11 = (s32[512]{0:T(512)S(1)}, s32[512]{0:T(512)}, u32[]{:S(2)}) copy-start(s32[512]{0:T(512)} %param.23) | copy-start | bytes 6148
  6.7 23.0 %copy-start.5 = (bf16[1,256,256]{2,1,0:T(8,128)(2,1)S(1)}, bf16[1,256,256]{2,1,0:T(8,128)(2,1)}, u32[]{:S(2)}) copy-start(bf16[1,256,256]{2,1,0:T(8,128)(2,1)} %param.19) | copy-start | bytes 393220
  7.8 226.5 %all-to-all-start = ((bf16[1,128,2,256]{3,2,0,1:T(2,128)(2,1)}), bf16[1,128,2,256]{3,2,0,1:T(2,128)(2,1)S(1)}, u32[]{:S(2)}, u32[]{:S(2)}) async-start(bf16[1,128,2,256]{3,2,0,1:T(2,128)(2,1)} %bitcast.6), calls=%async_computation | async-start | bytes 262144 | tf_op jit(solution)/shard_map/all_to_all | solution.py:48
  29.7 204.7 %copy-start.8 = (bf16[1,256,256]{2,1,0:T(8,128)(2,1)}, bf16[1,256,256]{2,1,0:T(8,128)(2,1)S(1)}, u32[]{:S(2)}) copy-start(bf16[1,256,256]{2,1,0:T(8,128)(2,1)S(1)} %neg.22) | copy-start | bytes 393220
  31.1 221.1 %copy-start.12 = (s32[2]{0:T(128)}, s32[2]{0:T(128)S(1)}, u32[]{:S(2)}) copy-start(s32[2]{0:T(128)S(1)} %pad_add_fusion) | copy-start | bytes 28
  35.5 198.9 %copy-start.15 = (bf16[1,256,256]{2,1,0:T(8,128)(2,1)S(1)}, bf16[1,256,256]{2,1,0:T(8,128)(2,1)}, u32[]{:S(2)}) copy-start(bf16[1,256,256]{2,1,0:T(8,128)(2,1)} %param.18) | copy-start | bytes 393220
  235.5 31.3 %all-to-all-start.1 = ((bf16[128,1,2,256]{3,2,1,0:T(2,128)(2,1)}), bf16[128,1,2,256]{3,2,1,0:T(2,128)(2,1)}, u32[]{:S(2)}, u32[]{:S(2)}) async-start(bf16[128,1,2,256]{3,2,1,0:T(2,128)(2,1)} %copy.50), calls=%async_computation.1 | async-start | bytes 262144 | tf_op jit(solution)/shard_map/all_to_all | solution.py:52
  252.2 16.2 %copy-start.4 = (bf16[1,2048,256]{2,1,0:T(8,128)(2,1)S(1)}, bf16[1,2048,256]{2,1,0:T(8,128)(2,1)}, u32[]{:S(2)}) copy-start(bf16[1,2048,256]{2,1,0:T(8,128)(2,1)} %param.14) | copy-start | bytes 3145732
  267.8 1.2 copy-start.14
  272.7 1.0 copy-start.1
  272.7 25.3 %copy-start.6 = (bf16[1,256,256]{2,1,0:T(8,128)(2,1)S(1)}, bf16[1,256,256]{2,1,0:T(8,128)(2,1)}, u32[]{:S(2)}) copy-start(bf16[1,256,256]{2,1,0:T(8,128)(2,1)} %param.19) | copy-start | bytes 393220
  272.7 25.3 %copy-start.9 = (bf16[1,256,256]{2,1,0:T(8,128)(2,1)S(1)}, bf16[1,256,256]{2,1,0:T(8,128)(2,1)}, u32[]{:S(2)}) copy-start(bf16[1,256,256]{2,1,0:T(8,128)(2,1)} %copy-done.8) | copy-start | bytes 393220
  272.7 25.4 %copy-start.16 = (bf16[1,256,256]{2,1,0:T(8,128)(2,1)S(1)}, bf16[1,256,256]{2,1,0:T(8,128)(2,1)}, u32[]{:S(2)}) copy-start(bf16[1,256,256]{2,1,0:T(8,128)(2,1)} %param.18) | copy-start | bytes 393220
  323.4 47.0 %all-to-all-start.4 = ((f32[512,1,256]{2,1,0:T(1,128)}), f32[512,1,256]{2,1,0:T(1,128)}, u32[]{:S(2)}, u32[]{:S(2)}) async-start(f32[512,1,256]{2,1,0:T(1,128)} %stack.13), calls=%async_computation.4 | async-start | bytes 1048576 | tf_op jit(solution)/shard_map/all_to_all | solution.py:140
  363.2 7.2 %copy-start.13 = (s32[2]{0:T(128)S(1)}, s32[2]{0:T(128)}, u32[]{:S(2)}) copy-start(s32[2]{0:T(128)} %copy-done.12) | copy-start | bytes 28
  363.2 8.6 %copy-start.7 = (bf16[256,256]{1,0:T(8,128)(2,1)S(1)}, bf16[256,256]{1,0:T(8,128)(2,1)}, u32[]{:S(2)}) copy-start(bf16[256,256]{1,0:T(8,128)(2,1)} %param.20) | copy-start | bytes 393220
  363.2 12.1 %copy-start.2 = (bf16[1,2048,256]{2,1,0:T(8,128)(2,1)S(1)}, bf16[1,2048,256]{2,1,0:T(8,128)(2,1)}, u32[]{:S(2)}) copy-start(bf16[1,2048,256]{2,1,0:T(8,128)(2,1)} %copy-done.1) | copy-start | bytes 3145732
